TPU v7x, 32 devices: a whole 2x2x4 slice. The times are simulated.
32 devices in a mesh: frames: 8 (over y, x, core), pos: 4 (over z).
Axes of the slice: x: 2, y: 2, z: 4, core: 2. Of those that a mesh axis runs over, the one named last changes fastest.
Arguments:
- frames_in: bfloat16 [512, 16, 1024], P(('frames', 'pos')), may hold values from -6 to 6
- frame_valid: int32 [512], P(('frames', 'pos')), may hold values 0 or 1
- last_position: int32 [512], P(('frames', 'pos')), may hold values from 0 to 15
- weight_qkv: bfloat16 [16, 1024, 3072], P('pos', 'frames'), may hold values from -0.1875 to 0.1875
- weight_out: bfloat16 [16, 1024, 1024], P('pos', 'frames'), may hold values from -0.5 to 0.5
- weight_ffn: bfloat16 [16, 1024, 5632], P('pos', 'frames'), may hold values from -0.1875 to 0.1875
- weight_down: bfloat16 [16, 2816, 1024], P('pos', 'frames'), may hold values from -0.109375 to 0.109375
- gain_attn: bfloat16 [16, 1024], P('pos', 'frames'), may hold values from 0.5 to 1.5
- gain_ffn: bfloat16 [16, 1024], P('pos', 'frames'), may hold values from 0.5 to 1.5
- grad_out: bfloat16 [512, 16, 1024], P(('frames', 'pos')), may hold values from -6 to 6
Outputs:
- output: bfloat16 [512, 16, 1024], P(('frames', 'pos'))
- grad_input: bfloat16 [512, 16, 1024], P(('frames', 'pos'))
- grad_qkv: float32 [16, 1024, 3072], P('pos', 'frames')
- grad_wout: float32 [16, 1024, 1024], P('pos', 'frames')
- grad_ffn: float32 [16, 1024, 5632], P('pos', 'frames')
- grad_down: float32 [16, 2816, 1024], P('pos', 'frames')
- grad_gain_attn: float32 [16, 1024], P('pos', 'frames')
- grad_gain_ffn: float32 [16, 1024], P('pos', 'frames')
All inputs are finite; a program needn't handle non-finite values. No bound on the sum of `frame_valid` on one device may be relied on, other than what follows from the above.
Results may differ from a plain program's by a relative error of at most 0.015.
Values may be sent and summed in bfloat16 or wider, within the bound.
No kernel may reach another device: no remote copies, remote signals or barrier semaphores. Data moves between devices by JAX's collectives and lax.ppermute only.
A program may use at most 384 MiB of HBM per device.

v0:
```python
import jax
import jax.numpy as jnp
from jax import lax
from jax.sharding import PartitionSpec as P

HEADS = 16
HEAD = 64
FF = 2816
EPSILON = 1e-06
NEGATIVE = -1e30


def rms_forward(values, gain_row):
    inverse = lax.rsqrt(jnp.mean(values * values, axis=-1, keepdims=True) + EPSILON)
    normed = values * inverse
    return (normed * gain_row[None], normed, inverse)


def rms_backward(upstream, normed, inverse, gain_row):
    scaled = upstream * gain_row[None]
    row_inner = jnp.mean(scaled * normed, axis=-1, keepdims=True)
    return (inverse * (scaled - normed * row_inner), jnp.sum(upstream * normed, axis=0))


def project(pattern, left_side, right_side):
    return jnp.einsum(pattern, left_side, right_side, preferred_element_type=jnp.float32)


def split_heads(qkv_frames):
    frames = qkv_frames.shape[0]
    length = qkv_frames.shape[1]
    pieces = qkv_frames.reshape(frames, length, 3, HEADS, HEAD)
    return (pieces[:, :, 0], pieces[:, :, 1], pieces[:, :, 2])


def masked_scores(query, key_part):
    raw_scores = project("fqhe,fkhe->fhqk", query, key_part) * HEAD ** (-0.5)
    length = raw_scores.shape[-1]
    allowed = lax.broadcasted_iota(jnp.int32, (length, length), 0) >= lax.broadcasted_iota(
        jnp.int32, (length, length), 1
    )
    return jnp.where(allowed, raw_scores, NEGATIVE)


def on_device(
    frames_in,
    frame_valid,
    last_position,
    weight_qkv,
    weight_out,
    weight_ffn,
    weight_down,
    gain_attn,
    gain_ffn,
    grad_out,
):
    scale = HEAD ** (-0.5)
    slot_index = lax.broadcasted_iota(jnp.int32, (frames_in.shape[0], frames_in.shape[1]), 1)
    live_mask = (frame_valid[:, None] > 0) & (slot_index <= last_position[:, None])
    pos_rows = lax.all_to_all(frames_in, "pos", split_axis=1, concat_axis=0, tiled=True)
    full_qkv, full_out, full_gain_a = (
        lax.all_gather(weight_qkv, "frames", axis=1, tiled=True),
        lax.all_gather(weight_out, "frames", axis=1, tiled=True),
        lax.all_gather(gain_attn, "frames", axis=1, tiled=True),
    )
    gain_one = full_gain_a.astype(jnp.float32)
    residual = pos_rows.astype(jnp.float32)
    scaled_one, normed_one, inverse_one = rms_forward(residual, gain_one)
    normed_one_low = scaled_one.astype(jnp.bfloat16)
    qkv_rows = project("rpd,pde->rpe", normed_one_low, full_qkv).astype(jnp.bfloat16)
    qkv_frames = lax.all_to_all(qkv_rows, "pos", split_axis=0, concat_axis=1, tiled=True)
    query, key_part, value_part = split_heads(qkv_frames)
    scores = masked_scores(query, key_part)
    row_top = jnp.max(scores, axis=-1, keepdims=True)
    exponent = jnp.exp(scores - row_top)
    row_total = jnp.sum(exponent, axis=-1, keepdims=True)
    log_total = row_top + jnp.log(row_total)
    attend_low = (exponent / row_total).astype(jnp.bfloat16)
    mixed_heads = project("fhqk,fkhe->fqhe", attend_low, value_part)
    mixed_low = mixed_heads.reshape(frames_in.shape).astype(jnp.bfloat16)
    mixed_rows = lax.all_to_all(mixed_low, "pos", split_axis=1, concat_axis=0, tiled=True)
    middle = residual + project("rpd,pde->rpe", mixed_rows, full_out)
    full_ffn, full_down, full_gain_f = (
        lax.all_gather(weight_ffn, "frames", axis=1, tiled=True),
        lax.all_gather(weight_down, "frames", axis=1, tiled=True),
        lax.all_gather(gain_ffn, "frames", axis=1, tiled=True),
    )
    gain_two = full_gain_f.astype(jnp.float32)
    scaled_two, normed_two, inverse_two = rms_forward(middle, gain_two)
    normed_two_low = scaled_two.astype(jnp.bfloat16)
    gate_up = project("rpd,pde->rpe", normed_two_low, full_ffn)
    gate = gate_up[..., :FF]
    upward = gate_up[..., FF:]
    gate_sig = jax.nn.sigmoid(gate)
    hidden = (gate * gate_sig * upward).astype(jnp.bfloat16)
    result = middle + project("rpf,pfd->rpd", hidden, full_down)
    result_frames = lax.all_to_all(
        result.astype(jnp.bfloat16), "pos", split_axis=0, concat_axis=1, tiled=True
    )
    output = jnp.where(live_mask[:, :, None], result_frames, jnp.zeros_like(result_frames))
    upstream = jnp.where(live_mask[:, :, None], grad_out, jnp.zeros_like(grad_out))
    upstream_rows = lax.all_to_all(upstream, "pos", split_axis=1, concat_axis=0, tiled=True)
    back_ffn, back_down = (
        lax.all_gather(weight_ffn, "frames", axis=1, tiled=True),
        lax.all_gather(weight_down, "frames", axis=1, tiled=True),
    )
    grad_hidden = project("rpd,pfd->rpf", upstream_rows, back_down)
    term_down = project("rpf,rpd->pfd", hidden, upstream_rows)
    grad_upward = grad_hidden * gate * gate_sig
    grad_gate = grad_hidden * upward * gate_sig * (1.0 + gate * (1.0 - gate_sig))
    grad_gate_up = jnp.concatenate([grad_gate, grad_upward], axis=-1).astype(jnp.bfloat16)
    grad_normed_two = project("rpe,pde->rpd", grad_gate_up, back_ffn)
    term_ffn = project("rpd,rpe->pde", normed_two_low, grad_gate_up)
    grad_middle_norm, term_gain_f = rms_backward(grad_normed_two, normed_two, inverse_two, gain_two)
    grad_middle = upstream_rows.astype(jnp.float32) + grad_middle_norm
    sum_ffn, sum_down, sum_gain_f = (
        lax.psum_scatter(
            term_ffn.astype(jnp.bfloat16), "frames", scatter_dimension=1, tiled=True
        ).astype(jnp.float32),
        lax.psum_scatter(
            term_down.astype(jnp.bfloat16), "frames", scatter_dimension=1, tiled=True
        ).astype(jnp.float32),
        lax.psum_scatter(
            term_gain_f.astype(jnp.bfloat16), "frames", scatter_dimension=1, tiled=True
        ).astype(jnp.float32),
    )
    back_qkv, back_out = (
        lax.all_gather(weight_qkv, "frames", axis=1, tiled=True),
        lax.all_gather(weight_out, "frames", axis=1, tiled=True),
    )
    grad_branch = grad_middle.astype(jnp.bfloat16)
    grad_mixed = project("rpe,pde->rpd", grad_branch, back_out).astype(jnp.bfloat16)
    term_out = project("rpd,rpe->pde", mixed_rows, grad_branch)
    grad_mixed_frames = lax.all_to_all(grad_mixed, "pos", split_axis=0, concat_axis=1, tiled=True)
    grad_heads = grad_mixed_frames.reshape(query.shape)
    again_scores = masked_scores(query, key_part)
    attend = jnp.exp(again_scores - log_total)
    grad_value = project("fhqk,fqhe->fkhe", attend.astype(jnp.bfloat16), grad_heads)
    grad_attend = project("fqhe,fkhe->fhqk", grad_heads, value_part)
    row_inner = jnp.sum(attend * grad_attend, axis=-1, keepdims=True)
    grad_scores = (attend * (grad_attend - row_inner)).astype(jnp.bfloat16)
    grad_query = project("fhqk,fkhe->fqhe", grad_scores, key_part) * scale
    grad_key = project("fhqk,fqhe->fkhe", grad_scores, query) * scale
    grad_qkv_frames = (
        jnp.stack([grad_query, grad_key, grad_value], axis=2)
        .reshape(qkv_frames.shape)
        .astype(jnp.bfloat16)
    )
    grad_qkv_rows = lax.all_to_all(grad_qkv_frames, "pos", split_axis=1, concat_axis=0, tiled=True)
    grad_normed_one = project("rpe,pde->rpd", grad_qkv_rows, back_qkv)
    term_qkv = project("rpd,rpe->pde", normed_one_low, grad_qkv_rows)
    grad_input_norm, term_gain_a = rms_backward(grad_normed_one, normed_one, inverse_one, gain_one)
    grad_rows = (grad_middle + grad_input_norm).astype(jnp.bfloat16)
    grad_frames = lax.all_to_all(grad_rows, "pos", split_axis=0, concat_axis=1, tiled=True)
    sum_qkv, sum_out, sum_gain_a = (
        lax.psum_scatter(
            term_qkv.astype(jnp.bfloat16), "frames", scatter_dimension=1, tiled=True
        ).astype(jnp.float32),
        lax.psum_scatter(
            term_out.astype(jnp.bfloat16), "frames", scatter_dimension=1, tiled=True
        ).astype(jnp.float32),
        lax.psum_scatter(
            term_gain_a.astype(jnp.bfloat16), "frames", scatter_dimension=1, tiled=True
        ).astype(jnp.float32),
    )
    return (output, grad_frames, sum_qkv, sum_out, sum_ffn, sum_down, sum_gain_a, sum_gain_f)


def solution(mesh):
    placed = (
        P(("frames", "pos"), None, None),
        P(("frames", "pos")),
        P(("frames", "pos")),
        P("pos", "frames", None),
        P("pos", "frames", None),
        P("pos", "frames", None),
        P("pos", "frames", None),
        P("pos", "frames"),
        P("pos", "frames"),
        P(("frames", "pos"), None, None),
    )
    return jax.shard_map(
        on_device,
        mesh=mesh,
        in_specs=placed,
        out_specs=(
            P(("frames", "pos"), None, None),
            P(("frames", "pos"), None, None),
            P("pos", "frames", None),
            P("pos", "frames", None),
            P("pos", "frames", None),
            P("pos", "frames", None),
            P("pos", "frames"),
            P("pos", "frames"),
        ),
        check_vma=False,
    )
```

profile of v0, /device:TPU:0, one launch (start us, length us, event | category | flops | bytes accessed | tf_op | source)
XLA Modules:
  0.0 1377.5 jit_solution(14971009679618732410)
XLA Ops:
  17.4 8.9 all_gather.22
  32.6 105.4 %all-gather.5.cloned.1.call-done = bf16[4,1024,3072]{2,1,0:T(8,128)(2,1)} async-done(((bf16[4,128,3072]{2,1,0:T(8,128)(2,1)}), bf16[4,1024,3072]{2,1,0:T(8,128)(2,1)}) %all-gather.5.cloned.1.call-update) | async-done | bytes 25165840 | tf_op jit(solution)/shard_map/all_gather | solution.py:62
  138.0 12.6 fusion
  158.8 36.3 %all-to-all-done.1 = bf16[64,4,3072]{2,1,0:T(4,128)(2,1)} async-done(((bf16[64,4,3072]{2,1,0:T(4,128)(2,1)}), bf16[64,4,3072]{2,1,0:T(4,128)(2,1)}, u32[]{:S(2)}, u32[]{:S(2)}) %all-to-all-start.1) | async-done | bytes 1572896 | tf_op jit(solution)/shard_map/all_to_all | solution.py:71
  221.1 9.2 all_gather.25
  240.8 169.6 %all-gather.9.cloned.1.call-done = bf16[4,1024,5632]{2,1,0:T(8,128)(2,1)} async-done(((bf16[4,128,5632]{2,1,0:T(8,128)(2,1)}), bf16[4,1024,5632]{2,1,0:T(8,128)(2,1)}) %all-gather.9.cloned.1.call-update) | async-done | bytes 46137360 | tf_op jit(solution)/shard_map/all_gather | solution.py:84
  410.4 23.7 %convolution_bitcast_fusion = f32[64,4,5632]{2,0,1:T(8,128)} fusion(bf16[4,1024,5632]{2,1,0:T(8,128)(2,1)} %all-gather.9.cloned.1.call-done, f32[64,4,1024]{2,0,1:T(8,128)S(1)} %get-tuple-element.29, f32[4,1024]{1,0:T(4,128)S(1)} %convert_element_type.128, f32[64,4]{0,1:T(4,128)S(1)} %add_rsqrt_fusion.1), kind=kOutput, calls=%fused_computation.3 | convolution fusion | flops 2953576448 | bytes 52970496 | tf_op jit(solution)/shard_map/rpd,pde->rpe/dot_general | solution.py:26
  434.1 94.5 %all-gather.11.cloned.1.call-done = bf16[4,2816,1024]{2,1,0:T(8,128)(2,1)} async-done(((bf16[4,352,1024]{2,1,0:T(8,128)(2,1)}), bf16[4,2816,1024]{2,1,0:T(8,128)(2,1)}) %all-gather.11.cloned.1.call-update) | async-done | bytes 23068688 | tf_op jit(solution)/shard_map/all_gather | solution.py:85
  528.7 14.3 %multiply_convert_fusion.1 = (bf16[64,4,2816]{2,0,1:T(8,128)(2,1)}, bf16[64,4,2816]{2,0,1:T(8,128)(2,1)}, bf16[64,4,2816]{2,0,1:T(8,128)(2,1)S(1)}) fusion(f32[64,4,5632]{2,0,1:T(8,128)} %convolution_bitcast_fusion, bf16[64,4,1024]{2,0,1:T(8,128)(2,1)} %bitcast.141, bf16[4,2816,1024]{2,1,0:T(8,128)(2,1)} %all-gather.11.cloned.1.call-done), kind=kOutput, calls=%fused_computation.11 | convolution fusion | flops 1487929344 | bytes 33685504 | tf_op jit(solution)/shard_map/rpd,pfd->rpf/dot_general | solution.py:26
  542.9 21.8 %multiply_reduce_fusion.1 = (bf16[4,1024]{1,0:T(4,128)(2,1)}, f32[64,4]{0,1:T(4,128)}, f32[64,4,1024]{2,0,1:T(8,128)}) fusion(f32[64,4,1024]{2,0,1:T(8,128)S(1)} %get-tuple-element.29, f32[64,4]{0,1:T(4,128)} %copy-done.15, f32[4,1024]{1,0:T(4,128)S(1)} %convert_element_type.128, bf16[4,1024,5632]{2,1,0:T(8,128)(2,1)} %all-gather.9.cloned.1.call-done, ...), kind=kOutput, calls=%fused_computation.45 | convolution fusion | flops 2960125696 | bytes 51144704 | tf_op jit(solution)/shard_map/rpe,pde->rpd/dot_general | solution.py:26
  581.2 13.4 all-to-all-done.5
  621.5 34.9 %all-to-all-done.6 = bf16[16,16,3072]{2,0,1:T(8,128)(2,1)} async-done(((bf16[16,16,3072]{2,0,1:T(8,128)(2,1)}), bf16[16,16,3072]{2,0,1:T(8,128)(2,1)}, u32[]{:S(2)}, u32[]{:S(2)}) %all-to-all-start.6) | async-done | bytes 1572896 | tf_op jit(solution)/shard_map/all_to_all | solution.py:149
  659.1 14.5 %multiply_reduce_fusion.2 = (bf16[4,1024]{1,0:T(4,128)(2,1)}, f32[64,4]{0,1:T(4,128)}, f32[64,4,1024]{2,0,1:T(8,128)}) fusion(f32[64,4,1024]{2,0,1:T(8,128)S(1)} %bitcast_multiply_fusion, f32[4,1024]{1,0:T(4,128)} %copy-done.12, bf16[64,4,3072]{2,0,1:T(8,128)(2,1)} %bitcast.135, bf16[4,1024,3072]{2,1,0:T(8,128)(2,1)} %all-gather.5.cloned.1.call-done), kind=kOutput, calls=%fused_computation.46 | convolution fusion | flops 1611919104 | bytes 28861440 | tf_op jit(solution)/shard_map/rpe,pde->rpd/dot_general | solution.py:26
  675.4 7.2 convolution_convert_fusion.3
  682.7 12.0 convolution_convert_fusion.2
  694.8 13.3 convolution_convert_fusion.1
  708.8 24.2 %convolution_convert_fusion = bf16[4,1024,5632]{2,1,0:T(8,128)(2,1)} fusion(bf16[64,4,2816]{2,0,1:T(8,128)(2,1)} %get-tuple-element.21, bf16[64,4,2816]{2,0,1:T(8,128)(2,1)} %get-tuple-element.20, f32[64,4,1024]{2,0,1:T(8,128)S(1)} %get-tuple-element.29, f32[4,1024]{1,0:T(4,128)S(1)} %convert_element_type.128, f32[64,4]{0,1:T(4,128)S(1)} %copy-done.16), kind=kOutput, calls=%fused_computation | convolution fusion | flops 2982412288 | bytes 50086912 | tf_op jit(solution)/shard_map/rpd,rpe->pde/dot_general | solution.py:26
  733.0 12.4 fusion.11
  754.0 10.1 all-to-all-done.3
  771.9 9.7 all-to-all-done.7
  785.5 146.9 %reduce-scatter.17.cloned.1.call-done = bf16[4,352,1024]{2,1,0:T(8,128)(2,1)} async-done(((bf16[4,2816,1024]{2,1,0:T(8,128)(2,1)}), bf16[4,352,1024]{2,1,0:T(8,128)(2,1)}) %reduce-scatter.17.cloned.1.call-update) | async-done | bytes 2883600 | tf_op jit(solution)/shard_map/reduce_scatter | solution.py:120
  937.5 155.9 %reduce-scatter.11.cloned.1.call-done = bf16[4,128,3072]{2,1,0:T(8,128)(2,1)} async-done(((bf16[4,1024,3072]{2,1,0:T(8,128)(2,1)}), bf16[4,128,3072]{2,1,0:T(8,128)(2,1)}) %reduce-scatter.11.cloned.1.call-update) | async-done | bytes 3145744 | tf_op jit(solution)/shard_map/reduce_scatter | solution.py:156
  1098.8 262.9 %reduce-scatter.15.cloned.1.call-done = bf16[4,128,5632]{2,1,0:T(8,128)(2,1)} async-done(((bf16[4,1024,5632]{2,1,0:T(8,128)(2,1)}), bf16[4,128,5632]{2,1,0:T(8,128)(2,1)}) %reduce-scatter.15.cloned.1.call-update) | async-done | bytes 5767184 | tf_op jit(solution)/shard_map/reduce_scatter | solution.py:117
  1361.7 8.6 convert_element_type.145
  (153 shorter events, 140.0 us)
Async XLA Ops:
  7.2 130.8 %all-gather.5.cloned.1.call-start = ((), (), s32[]{:S(2)}) async-start(), calls=%async_computation.14 | async-start | bytes 28311552 | tf_op jit(solution)/shard_map/all_gather | solution.py:62
  7.9 227.6 %all-gather.7.cloned.1.call-start = ((), (), s32[]{:S(2)}) async-start(), calls=%async_computation.15 | async-start | bytes 9437184 | tf_op jit(solution)/shard_map/all_gather | solution.py:63
  8.7 401.7 %all-gather.9.cloned.1.call-start = ((), (), s32[]{:S(2)}) async-start(), calls=%async_computation.16 | async-start | bytes 51904512 | tf_op jit(solution)/shard_map/all_gather | solution.py:84
  9.4 519.3 %all-gather.11.cloned.1.call-start = ((), (), s32[]{:S(2)}) async-start(), calls=%async_computation.17 | async-start | bytes 25952256 | tf_op jit(solution)/shard_map/all_gather | solution.py:85
  11.1 20.8 %all-to-all-start = ((bf16[16,16,1024]{2,0,1:T(8,128)(2,1)}), bf16[16,16,1024]{2,0,1:T(8,128)(2,1)S(1)}, u32[]{:S(2)}, u32[]{:S(2)}) async-start(bf16[16,16,1024]{2,0,1:T(8,128)(2,1)} %copy.63), calls=%async_computation | async-start | bytes 1048576 | tf_op jit(solution)/shard_map/all_to_all | solution.py:60
  26.3 124.3 %copy-start.12 = (f32[4,1024]{1,0:T(4,128)}, f32[4,1024]{1,0:T(4,128)S(1)}, u32[]{:S(2)}) copy-start(f32[4,1024]{1,0:T(4,128)S(1)} %convert_element_type.120) | copy-start | bytes 49156
  32.3 105.7 %copy-start.21 = (f32[64,4]{0,1:T(4,128)}, f32[64,4]{0,1:T(4,128)S(1)}, u32[]{:S(2)}) copy-start(f32[64,4]{0,1:T(4,128)S(1)} %rsqrt.20) | copy-start | bytes 3076
  32.4 203.1 %copy-start.2 = (f32[16,4,4,1024]{3,0,1,2:T(8,128)}, f32[16,4,4,1024]{3,0,1,2:T(8,128)S(1)}, u32[]{:S(2)}) copy-start(f32[16,4,4,1024]{3,0,1,2:T(8,128)S(1)} %copy.64) | copy-start | bytes 3145732
  153.0 42.1 %all-to-all-start.1 = ((bf16[64,4,3072]{2,1,0:T(4,128)(2,1)}), bf16[64,4,3072]{2,1,0:T(4,128)(2,1)}, u32[]{:S(2)}, u32[]{:S(2)}) async-start(bf16[64,4,3072]{2,1,0:T(4,128)(2,1)} %copy.68), calls=%async_computation.1 | async-start | bytes 3145728 | tf_op jit(solution)/shard_map/all_to_all | solution.py:71
  157.7 50.1 %copy-start.22 = (pred[16,16]{0,1:T(8,128)(4,1)}, pred[16,16]{0,1:T(8,128)(4,1)S(1)}, u32[]{:S(2)}) copy-start(pred[16,16]{0,1:T(8,128)(4,1)S(1)} %fusion.21) | copy-start | bytes 772
  195.1 20.9 %all-to-all-start.4 = ((bf16[16,16,1024]{2,0,1:T(8,128)(2,1)}), bf16[16,16,1024]{2,0,1:T(8,128)(2,1)}, u32[]{:S(2)}, u32[]{:S(2)}) async-start(bf16[16,16,1024]{2,0,1:T(8,128)(2,1)} %copy_select_fusion), calls=%async_computation.4 | async-start | bytes 1048576 | tf_op jit(solution)/shard_map/all_to_all | solution.py:102
  216.0 18.7 %all-to-all-start.2 = ((bf16[16,16,1024]{2,0,1:T(8,128)(2,1)}), bf16[16,16,1024]{2,0,1:T(8,128)(2,1)S(1)}, u32[]{:S(2)}, u32[]{:S(2)}) async-start(bf16[16,16,1024]{2,0,1:T(8,128)(2,1)} %reshape.126), calls=%async_computation.2 | async-start | bytes 1048576 | tf_op jit(solution)/shard_map/all_to_all | solution.py:81
  240.8 193.3 %copy-start.15 = (f32[64,4]{0,1:T(4,128)}, f32[64,4]{0,1:T(4,128)S(1)}, u32[]{:S(2)}) copy-start(f32[64,4]{0,1:T(4,128)S(1)} %add_rsqrt_fusion.1) | copy-start | bytes 3076
  574.8 19.8 %all-to-all-start.5 = ((bf16[64,4,1024]{2,1,0:T(4,128)(2,1)}), bf16[64,4,1024]{2,1,0:T(4,128)(2,1)}, u32[]{:S(2)}, u32[]{:S(2)}) async-start(bf16[64,4,1024]{2,1,0:T(4,128)(2,1)} %copy.81), calls=%async_computation.5 | async-start | bytes 1048576 | tf_op jit(solution)/shard_map/all_to_all | solution.py:134
  615.4 41.0 %all-to-all-start.6 = ((bf16[16,16,3072]{2,0,1:T(8,128)(2,1)}), bf16[16,16,3072]{2,0,1:T(8,128)(2,1)}, u32[]{:S(2)}, u32[]{:S(2)}) async-start(bf16[16,16,3072]{2,0,1:T(8,128)(2,1)} %reshape.127), calls=%async_computation.6 | async-start | bytes 3145728 | tf_op jit(solution)/shard_map/all_to_all | solution.py:149
  619.8 147.8 %reduce-scatter.21.cloned.1.call-start = ((), (), s32[]{:S(2)}) async-start(), calls=%async_computation.23 | async-start | bytes 294912
  621.4 149.0 %reduce-scatter.19.cloned.1.call-start = ((), (), s32[]{:S(2)}) async-start(), calls=%async_computation.22 | async-start | bytes 294912
  675.2 107.5 %reduce-scatter.13.cloned.1.call-start = ((), (), s32[]{:S(2)}) async-start(), calls=%async_computation.19 | async-start | bytes 9437184 | tf_op jit(solution)/shard_map/reduce_scatter | solution.py:159
  682.6 249.8 %reduce-scatter.17.cloned.1.call-start = ((), (), s32[]{:S(2)}) async-start(), calls=%async_computation.21 | async-start | bytes 25952256 | tf_op jit(solution)/shard_map/reduce_scatter | solution.py:120
  694.7 398.6 %reduce-scatter.11.cloned.1.call-start = ((), (), s32[]{:S(2)}) async-start(), calls=%async_computation.18 | async-start | bytes 28311552 | tf_op jit(solution)/shard_map/reduce_scatter | solution.py:156
  708.1 653.6 %reduce-scatter.15.cloned.1.call-start = ((), (), s32[]{:S(2)}) async-start(), calls=%async_computation.20 | async-start | bytes 51904512 | tf_op jit(solution)/shard_map/reduce_scatter | solution.py:117
  746.6 17.5 %all-to-all-start.3 = ((bf16[64,4,1024]{2,1,0:T(4,128)(2,1)}), bf16[64,4,1024]{2,1,0:T(4,128)(2,1)S(1)}, u32[]{:S(2)}, u32[]{:S(2)}) async-start(bf16[64,4,1024]{2,1,0:T(4,128)(2,1)} %copy.77), calls=%async_computation.3 | async-start | bytes 1048576 | tf_op jit(solution)/shard_map/all_to_all | solution.py:97
  750.8 18.4 %copy-start.23 = (pred[16,16]{0,1:T(8,128)(4,1)S(1)}, pred[16,16]{0,1:T(8,128)(4,1)}, u32[]{:S(2)}) copy-start(pred[16,16]{0,1:T(8,128)(4,1)} %copy-done.22) | copy-start | bytes 772
  764.1 17.4 %all-to-all-start.7 = ((bf16[64,4,1024]{2,1,0:T(4,128)(2,1)}), bf16[64,4,1024]{2,1,0:T(4,128)(2,1)S(1)}, u32[]{:S(2)}, u32[]{:S(2)}) async-start(bf16[64,4,1024]{2,1,0:T(4,128)(2,1)} %copy.89), calls=%async_computation.7 | async-start | bytes 1048576 | tf_op jit(solution)/shard_map/all_to_all | solution.py:154
  (22 other events, 106.7 us)
Sparse Core Ops, SparseCore 0:
  9.9 128.0 all-gather.4
  139.9 54.3 all-gather.6
  196.2 214.1 all-gather.8
  412.2 116.4 all-gather.10
  623.3 34.0 reduce-scatter.20
  675.3 31.7 reduce-scatter.18
  711.1 71.2 reduce-scatter.12
  786.5 145.8 reduce-scatter.16
  936.5 156.8 reduce-scatter.10
  1097.3 264.3 reduce-scatter.14
where the time goes:
time: 1380 us
  waiting for transfers between devices  1050 us (76%)
  matrix products  177 us (13%)
  local copies, waits for them, and re-layouts  46.6 us (3%)
  starting transfers between devices  37.2 us (3%)
  other arithmetic  33.2 us (2%)
  blocking collectives  18.1 us (1%)
  between operations  15.1 us (1%)
    reduce_scatter x1, waiting for transfers between devices, on_device(): lax.psum_scatter(term_ffn.astype(jnp.bfloat16), 'frames', scatter_dimensi...  263 us
    dot_general x18, matrix products, project(): jnp.einsum(pattern, left_side, right_side, preferred_element_type=jnp.flo...  177 us
    all_gather x1, waiting for transfers between devices, on_device(): lax.all_gather(weight_ffn, 'frames', axis=1, tiled=True)  170 us
    reduce_scatter x1, waiting for transfers between devices, on_device(): lax.psum_scatter(term_qkv.astype(jnp.bfloat16), 'frames', scatter_dimensi...  156 us
    reduce_scatter x1, waiting for transfers between devices, on_device(): lax.psum_scatter(term_down.astype(jnp.bfloat16), 'frames', scatter_dimens...  147 us
    all_gather x1, waiting for transfers between devices, on_device(): lax.all_gather(weight_qkv, 'frames', axis=1, tiled=True)  105 us
    all_gather x1, waiting for transfers between devices, on_device(): lax.all_gather(weight_down, 'frames', axis=1, tiled=True)  94.5 us
    all_to_all x1, waiting for transfers between devices, on_device(): lax.all_to_all(qkv_rows, 'pos', split_axis=0, concat_axis=1, tiled=True)  36.3 us
  transfers between devices with their start and end apart: 18, of which 13 were waited for; matrix products, arithmetic and copies ran while one was open for 13% of the time, Pallas kernels for 0%

commit v1 on v0

--- a/solution.py
+++ b/solution.py
@@ -8,6 +8,19 @@
 FF = 2816
 EPSILON = 1e-06
 NEGATIVE = -1e30
+
+
+def gather_around(x, axis, dim):
+    ways = lax.axis_size(axis)
+    up = [(d, (d + 1) % ways) for d in range(ways)]
+    down = [(d, (d - 1) % ways) for d in range(ways)]
+    earlier, later = ([x], [x])
+    for _ in range(ways // 2):
+        earlier.append(lax.ppermute(earlier[-1], axis, up))
+    for _ in range((ways - 1) // 2):
+        later.append(lax.ppermute(later[-1], axis, down))
+    line = jnp.concatenate([*earlier[::-1], *later[1:]], axis=dim)
+    return jnp.roll(line, (lax.axis_index(axis) - ways // 2) * x.shape[dim], axis=dim)
 
 
 def rms_forward(values, gain_row):
@@ -82,7 +95,7 @@
     middle = residual + project("rpd,pde->rpe", mixed_rows, full_out)
     full_ffn, full_down, full_gain_f = (
         lax.all_gather(weight_ffn, "frames", axis=1, tiled=True),
-        lax.all_gather(weight_down, "frames", axis=1, tiled=True),
+        gather_around(weight_down, "frames", 1),
         lax.all_gather(gain_ffn, "frames", axis=1, tiled=True),
     )
     gain_two = full_gain_f.astype(jnp.float32)

time: 1380 us -> 1490 us (1.080)
  local copies, waits for them, and re-layouts: 46.6 us -> 98.2 us
  waiting for transfers between devices: 1050 us -> 1090 us
    ppermute x0 -> x7, waiting for transfers between devices: none -> 340 us  [the longest x4 332 us: gather_around(): earlier.append(lax.ppermute(earlier[-1], axis, up))]
    reduce_scatter x1, waiting for transfers between devices: 147 us -> 0.01 us  [on_device(): lax.psum_scatter(term_down.astype(jnp.bfloat16), 'frames', scatter_dimens...]
    reduce_scatter x1, waiting for transfers between devices: 156 us -> 11.6 us  [on_device(): lax.psum_scatter(term_qkv.astype(jnp.bfloat16), 'frames', scatter_dimensi...]
    unnamed x63 -> x90, local copies, waits for them, and re-layouts: 8.73 us -> 56.6 us
  transfers between devices with their start and end apart: 18 -> 25, of which waited for: 13 -> 18; matrix products, arithmetic and copies ran while one was open for 13% -> 15% of each run, Pallas kernels for 0% -> 0%
where the time goes in v1:
time: 1490 us; the launch traced here: 1480 us
  waiting for transfers between devices  1090 us (73%)
  matrix products  179 us (12%)
  local copies, waits for them, and re-layouts  98.2 us (7%)
  starting transfers between devices  46 us (3%)
  other arithmetic  33.2 us (2%)
  blocking collectives  18.3 us (1%)
  between operations  14.9 us (1%)
    ppermute x4, waiting for transfers between devices, gather_around(): earlier.append(lax.ppermute(earlier[-1], axis, up))  332 us
    reduce_scatter x1, waiting for transfers between devices, on_device(): lax.psum_scatter(term_ffn.astype(jnp.bfloat16), 'frames', scatter_dimensi...  263 us
    dot_general x18, matrix products, project(): jnp.einsum(pattern, left_side, right_side, preferred_element_type=jnp.flo...  179 us
    all_gather x1, waiting for transfers between devices, on_device(): lax.all_gather(weight_ffn, 'frames', axis=1, tiled=True)  169 us
    all_gather x1, waiting for transfers between devices, on_device(): lax.all_gather(weight_qkv, 'frames', axis=1, tiled=True)  105 us
    all_gather x1, waiting for transfers between devices, on_device(): lax.all_gather(weight_down, 'frames', axis=1, tiled=True)  94.5 us
    unnamed x90, local copies, waits for them, and re-layouts  56.6 us
    all_to_all x1, waiting for transfers between devices, on_device(): lax.all_to_all(qkv_rows, 'pos', split_axis=0, concat_axis=1, tiled=True)  36.3 us
  transfers between devices with their start and end apart: 25, of which 18 were waited for; matrix products, arithmetic and copies ran while one was open for 15% of the time, Pallas kernels for 0%

profile of v1, /device:TPU:0, one launch (start us, length us, event | category | flops | bytes accessed | tf_op | source)
XLA Modules:
  0.0 1481.5 jit_solution(7764616758972777838)
XLA Ops:
  17.4 8.9 all_gather.21
  32.6 105.4 %all-gather.5.cloned.1.call-done = bf16[4,1024,3072]{2,1,0:T(8,128)(2,1)} async-done(((bf16[4,128,3072]{2,1,0:T(8,128)(2,1)}), bf16[4,1024,3072]{2,1,0:T(8,128)(2,1)}) %all-gather.5.cloned.1.call-update) | async-done | bytes 25165840 | tf_op jit(solution)/shard_map/all_gather | solution.py:75
  138.0 12.6 fusion.2
  158.8 36.3 %all-to-all-done.1 = bf16[64,4,3072]{2,1,0:T(4,128)(2,1)} async-done(((bf16[64,4,3072]{2,1,0:T(4,128)(2,1)}), bf16[64,4,3072]{2,1,0:T(4,128)(2,1)}, u32[]{:S(2)}, u32[]{:S(2)}) %all-to-all-start.1) | async-done | bytes 1572896 | tf_op jit(solution)/shard_map/all_to_all | solution.py:84
  221.2 9.4 all_gather.24
  241.0 169.4 %all-gather.9.cloned.1.call-done = bf16[4,1024,5632]{2,1,0:T(8,128)(2,1)} async-done(((bf16[4,128,5632]{2,1,0:T(8,128)(2,1)}), bf16[4,1024,5632]{2,1,0:T(8,128)(2,1)}) %all-gather.9.cloned.1.call-update) | async-done | bytes 46137360 | tf_op jit(solution)/shard_map/all_gather | solution.py:97
  410.4 23.7 %convolution_bitcast_fusion = f32[64,4,5632]{2,0,1:T(8,128)} fusion(bf16[4,1024,5632]{2,1,0:T(8,128)(2,1)} %all-gather.9.cloned.1.call-done, f32[64,4,1024]{2,0,1:T(8,128)S(1)} %get-tuple-element.29, f32[4,1024]{1,0:T(4,128)S(1)} %convert_element_type.128, f32[64,4]{0,1:T(4,128)S(1)} %add_rsqrt_fusion.1), kind=kOutput, calls=%fused_computation.5 | convolution fusion | flops 2953576448 | bytes 52970496 | tf_op jit(solution)/shard_map/rpd,pde->rpe/dot_general | solution.py:39
  434.1 94.5 %all-gather.11.cloned.1.call-done = bf16[4,2816,1024]{2,1,0:T(8,128)(2,1)} async-done(((bf16[4,352,1024]{2,1,0:T(8,128)(2,1)}), bf16[4,2816,1024]{2,1,0:T(8,128)(2,1)}) %all-gather.11.cloned.1.call-update) | async-done | bytes 23068688 | tf_op jit(solution)/shard_map/all_gather | solution.py:118
  528.7 14.2 multiply_convert_fusion.1
  542.9 21.8 %multiply_reduce_fusion.1 = (bf16[4,1024]{1,0:T(4,128)(2,1)}, f32[64,4]{0,1:T(4,128)}, f32[64,4,1024]{2,0,1:T(8,128)}) fusion(f32[64,4,1024]{2,0,1:T(8,128)S(1)} %get-tuple-element.29, f32[64,4]{0,1:T(4,128)} %copy-done.21, f32[4,1024]{1,0:T(4,128)S(1)} %convert_element_type.128, bf16[4,1024,5632]{2,1,0:T(8,128)(2,1)} %all-gather.9.cloned.1.call-done, ...), kind=kOutput, calls=%fused_computation.45 | convolution fusion | flops 2960125696 | bytes 51144704 | tf_op jit(solution)/shard_map/rpe,pde->rpd/dot_general | solution.py:39
  581.1 13.4 all-to-all-done.5
  621.5 34.9 %all-to-all-done.6 = bf16[16,16,3072]{2,0,1:T(8,128)(2,1)} async-done(((bf16[16,16,3072]{2,0,1:T(8,128)(2,1)}), bf16[16,16,3072]{2,0,1:T(8,128)(2,1)}, u32[]{:S(2)}, u32[]{:S(2)}) %all-to-all-start.6) | async-done | bytes 1572896 | tf_op jit(solution)/shard_map/all_to_all | solution.py:162
  659.1 14.5 multiply_reduce_fusion.2
  682.7 11.9 convolution_convert_fusion.2
  694.8 13.3 convolution_convert_fusion.1
  708.7 24.2 %convolution_convert_fusion = bf16[4,1024,5632]{2,1,0:T(8,128)(2,1)} fusion(bf16[64,4,2816]{2,0,1:T(8,128)(2,1)} %get-tuple-element.21, bf16[64,4,2816]{2,0,1:T(8,128)(2,1)} %get-tuple-element.20, f32[64,4,1024]{2,0,1:T(8,128)S(1)} %get-tuple-element.29, f32[4,1024]{1,0:T(4,128)S(1)} %convert_element_type.128, f32[64,4]{0,1:T(4,128)S(1)} %copy-done.22), kind=kOutput, calls=%fused_computation | convolution fusion | flops 2982412288 | bytes 50086912 | tf_op jit(solution)/shard_map/rpd,rpe->pde/dot_general | solution.py:39
  733.0 68.7 %collective-permute-done = bf16[4,352,1024]{2,1,0:T(8,128)(2,1)S(1)} collective-permute-done((bf16[4,352,1024]{2,1,0:T(8,128)(2,1)}, bf16[4,352,1024]{2,1,0:T(8,128)(2,1)S(1)}, u32[]{:S(2)}, u32[]{:S(2)}) %collective-permute-start) | collective-permute-done | bytes 2883616 | tf_op jit(solution)/shard_map/ppermute | solution.py:19
  805.9 84.7 %collective-permute-done.1 = bf16[4,352,1024]{2,1,0:T(8,128)(2,1)S(1)} collective-permute-done((bf16[4,352,1024]{2,1,0:T(8,128)(2,1)S(1)}, bf16[4,352,1024]{2,1,0:T(8,128)(2,1)S(1)}, u32[]{:S(2)}, u32[]{:S(2)}) %collective-permute-start.1) | collective-permute-done | bytes 2883616 | tf_op jit(solution)/shard_map/ppermute | solution.py:19
  897.7 109.6 %collective-permute-done.2 = bf16[4,352,1024]{2,1,0:T(8,128)(2,1)} collective-permute-done((bf16[4,352,1024]{2,1,0:T(8,128)(2,1)S(1)}, bf16[4,352,1024]{2,1,0:T(8,128)(2,1)}, u32[]{:S(2)}, u32[]{:S(2)}) %collective-permute-start.2) | collective-permute-done | bytes 2883616 | tf_op jit(solution)/shard_map/ppermute | solution.py:19
  1015.5 69.4 %collective-permute-done.3 = bf16[4,352,1024]{2,1,0:T(8,128)(2,1)} collective-permute-done((bf16[4,352,1024]{2,1,0:T(8,128)(2,1)}, bf16[4,352,1024]{2,1,0:T(8,128)(2,1)}, u32[]{:S(2)}, u32[]{:S(2)}) %collective-permute-start.3) | collective-permute-done | bytes 2883616 | tf_op jit(solution)/shard_map/ppermute | solution.py:19
  1133.3 14.6 add_convert_fusion.1
  1186.1 11.6 reduce-scatter.11.cloned.1.call-done
  1203.1 262.8 %reduce-scatter.15.cloned.1.call-done = bf16[4,128,5632]{2,1,0:T(8,128)(2,1)} async-done(((bf16[4,1024,5632]{2,1,0:T(8,128)(2,1)}), bf16[4,128,5632]{2,1,0:T(8,128)(2,1)}) %reduce-scatter.15.cloned.1.call-update) | async-done | bytes 5767184 | tf_op jit(solution)/shard_map/reduce_scatter | solution.py:130
  1465.9 8.6 convert_element_type.145
  (195 shorter events, 228.2 us)
Async XLA Ops:
  7.2 130.8 %all-gather.5.cloned.1.call-start = ((), (), s32[]{:S(2)}) async-start(), calls=%async_computation.14 | async-start | bytes 28311552 | tf_op jit(solution)/shard_map/all_gather | solution.py:75
  7.9 227.9 %all-gather.7.cloned.1.call-start = ((), (), s32[]{:S(2)}) async-start(), calls=%async_computation.15 | async-start | bytes 9437184 | tf_op jit(solution)/shard_map/all_gather | solution.py:76
  8.7 401.7 %all-gather.9.cloned.1.call-start = ((), (), s32[]{:S(2)}) async-start(), calls=%async_computation.16 | async-start | bytes 51904512 | tf_op jit(solution)/shard_map/all_gather | solution.py:97
  9.4 519.2 %all-gather.11.cloned.1.call-start = ((), (), s32[]{:S(2)}) async-start(), calls=%async_computation.17 | async-start | bytes 25952256 | tf_op jit(solution)/shard_map/all_gather | solution.py:118
  11.1 20.8 %all-to-all-start = ((bf16[16,16,1024]{2,0,1:T(8,128)(2,1)}), bf16[16,16,1024]{2,0,1:T(8,128)(2,1)S(1)}, u32[]{:S(2)}, u32[]{:S(2)}) async-start(bf16[16,16,1024]{2,0,1:T(8,128)(2,1)} %copy.63), calls=%async_computation | async-start | bytes 1048576 | tf_op jit(solution)/shard_map/all_to_all | solution.py:73
  153.0 42.1 %all-to-all-start.1 = ((bf16[64,4,3072]{2,1,0:T(4,128)(2,1)}), bf16[64,4,3072]{2,1,0:T(4,128)(2,1)}, u32[]{:S(2)}, u32[]{:S(2)}) async-start(bf16[64,4,3072]{2,1,0:T(4,128)(2,1)} %copy.68), calls=%async_computation.1 | async-start | bytes 3145728 | tf_op jit(solution)/shard_map/all_to_all | solution.py:84
  195.1 21.1 %all-to-all-start.4 = ((bf16[16,16,1024]{2,0,1:T(8,128)(2,1)}), bf16[16,16,1024]{2,0,1:T(8,128)(2,1)}, u32[]{:S(2)}, u32[]{:S(2)}) async-start(bf16[16,16,1024]{2,0,1:T(8,128)(2,1)} %copy_select_fusion), calls=%async_computation.4 | async-start | bytes 1048576 | tf_op jit(solution)/shard_map/all_to_all | solution.py:115
  216.2 18.7 %all-to-all-start.2 = ((bf16[16,16,1024]{2,0,1:T(8,128)(2,1)}), bf16[16,16,1024]{2,0,1:T(8,128)(2,1)S(1)}, u32[]{:S(2)}, u32[]{:S(2)}) async-start(bf16[16,16,1024]{2,0,1:T(8,128)(2,1)} %reshape.126), calls=%async_computation.2 | async-start | bytes 1048576 | tf_op jit(solution)/shard_map/all_to_all | solution.py:94
  574.7 19.8 %all-to-all-start.5 = ((bf16[64,4,1024]{2,1,0:T(4,128)(2,1)}), bf16[64,4,1024]{2,1,0:T(4,128)(2,1)}, u32[]{:S(2)}, u32[]{:S(2)}) async-start(bf16[64,4,1024]{2,1,0:T(4,128)(2,1)} %copy.81), calls=%async_computation.5 | async-start | bytes 1048576 | tf_op jit(solution)/shard_map/all_to_all | solution.py:147
  615.5 40.9 %all-to-all-start.6 = ((bf16[16,16,3072]{2,0,1:T(8,128)(2,1)}), bf16[16,16,3072]{2,0,1:T(8,128)(2,1)}, u32[]{:S(2)}, u32[]{:S(2)}) async-start(bf16[16,16,3072]{2,0,1:T(8,128)(2,1)} %reshape.127), calls=%async_computation.6 | async-start | bytes 3145728 | tf_op jit(solution)/shard_map/all_to_all | solution.py:162
  619.8 547.0 %reduce-scatter.21.cloned.1.call-start = ((), (), s32[]{:S(2)}) async-start(), calls=%async_computation.23 | async-start | bytes 294912
  621.5 548.1 %reduce-scatter.19.cloned.1.call-start = ((), (), s32[]{:S(2)}) async-start(), calls=%async_computation.22 | async-start | bytes 294912
  675.2 503.0 %reduce-scatter.13.cloned.1.call-start = ((), (), s32[]{:S(2)}) async-start(), calls=%async_computation.19 | async-start | bytes 9437184 | tf_op jit(solution)/shard_map/reduce_scatter | solution.py:172
  682.7 498.3 %reduce-scatter.17.cloned.1.call-start = ((), (), s32[]{:S(2)}) async-start(), calls=%async_computation.21 | async-start | bytes 25952256 | tf_op jit(solution)/shard_map/reduce_scatter | solution.py:133
  694.7 503.0 %reduce-scatter.11.cloned.1.call-start = ((), (), s32[]{:S(2)}) async-start(), calls=%async_computation.18 | async-start | bytes 28311552 | tf_op jit(solution)/shard_map/reduce_scatter | solution.py:169
  708.0 757.9 %reduce-scatter.15.cloned.1.call-start = ((), (), s32[]{:S(2)}) async-start(), calls=%async_computation.20 | async-start | bytes 51904512 | tf_op jit(solution)/shard_map/reduce_scatter | solution.py:130
  732.9 68.8 %collective-permute-start = (bf16[4,352,1024]{2,1,0:T(8,128)(2,1)}, bf16[4,352,1024]{2,1,0:T(8,128)(2,1)S(1)}, u32[]{:S(2)}, u32[]{:S(2)}) collective-permute-start(bf16[4,352,1024]{2,1,0:T(8,128)(2,1)} %param.16), channel_id=1, source_target_pairs={{0,4},{4,8},{8,12},{12,16},{16,20},{20,24},{24,28},{28,0},{1,5},{5... | collective-permute-start | bytes 8650760 | tf_op jit(solution)/shard_map/ppermute | solution.py:19
  803.2 87.4 %collective-permute-start.1 = (bf16[4,352,1024]{2,1,0:T(8,128)(2,1)S(1)}, bf16[4,352,1024]{2,1,0:T(8,128)(2,1)S(1)}, u32[]{:S(2)}, u32[]{:S(2)}) collective-permute-start(bf16[4,352,1024]{2,1,0:T(8,128)(2,1)S(1)} %collective-permute-done), channel_id=1, source_target_pairs={{0,4},{4,8},{8,12},{12,16},{16,20},{20,24},{24,28},{28,0},{1,5},{5... | collective-permute-start | bytes 8650760 | tf_op jit(solution)/shard_map/ppermute | solution.py:19
  803.2 90.2 %collective-permute-start.4 = (bf16[4,352,1024]{2,1,0:T(8,128)(2,1)}, bf16[4,352,1024]{2,1,0:T(8,128)(2,1)S(1)}, u32[]{:S(2)}, u32[]{:S(2)}) collective-permute-start(bf16[4,352,1024]{2,1,0:T(8,128)(2,1)} %param.16), channel_id=1, source_target_pairs={{0,28},{4,0},{8,4},{12,8},{16,12},{20,16},{24,20},{28,24},{1,29},{... | collective-permute-start | bytes 8650760 | tf_op jit(solution)/shard_map/ppermute | solution.py:21
  890.6 116.7 %collective-permute-start.2 = (bf16[4,352,1024]{2,1,0:T(8,128)(2,1)S(1)}, bf16[4,352,1024]{2,1,0:T(8,128)(2,1)}, u32[]{:S(2)}, u32[]{:S(2)}) collective-permute-start(bf16[4,352,1024]{2,1,0:T(8,128)(2,1)S(1)} %collective-permute-done.1), channel_id=1, source_target_pairs={{0,4},{4,8},{8,12},{12,16},{16,20},{20,24},{24,28},{28,0},{1,5},{5... | collective-permute-start | bytes 8650760 | tf_op jit(solution)/shard_map/ppermute | solution.py:19
  895.0 117.2 %collective-permute-start.5 = (bf16[4,352,1024]{2,1,0:T(8,128)(2,1)S(1)}, bf16[4,352,1024]{2,1,0:T(8,128)(2,1)}, u32[]{:S(2)}, u32[]{:S(2)}) collective-permute-start(bf16[4,352,1024]{2,1,0:T(8,128)(2,1)S(1)} %collective-permute-done.4), channel_id=1, source_target_pairs={{0,28},{4,0},{8,4},{12,8},{16,12},{20,16},{24,20},{28,24},{1,29},{... | collective-permute-start | bytes 8650760 | tf_op jit(solution)/shard_map/ppermute | solution.py:21
  1007.3 77.5 %collective-permute-start.3 = (bf16[4,352,1024]{2,1,0:T(8,128)(2,1)}, bf16[4,352,1024]{2,1,0:T(8,128)(2,1)}, u32[]{:S(2)}, u32[]{:S(2)}) collective-permute-start(bf16[4,352,1024]{2,1,0:T(8,128)(2,1)} %collective-permute-done.2), channel_id=1, source_target_pairs={{0,4},{4,8},{8,12},{12,16},{16,20},{20,24},{24,28},{28,0},{1,5},{5... | collective-permute-start | bytes 8650760 | tf_op jit(solution)/shard_map/ppermute | solution.py:19
  1012.2 94.9 %collective-permute-start.6 = (bf16[4,352,1024]{2,1,0:T(8,128)(2,1)}, bf16[4,352,1024]{2,1,0:T(8,128)(2,1)}, u32[]{:S(2)}, u32[]{:S(2)}) collective-permute-start(bf16[4,352,1024]{2,1,0:T(8,128)(2,1)} %collective-permute-done.5), channel_id=1, source_target_pairs={{0,28},{4,0},{8,4},{12,8},{16,12},{20,16},{24,20},{28,24},{1,29},{... | collective-permute-start | bytes 8650760 | tf_op jit(solution)/shard_map/ppermute | solution.py:21
  1149.2 14.0 all-to-all-start.3
  (35 other events, 964.9 us)
Sparse Core Ops, SparseCore 0:
  9.9 128.0 all-gather.4
  139.9 54.3 all-gather.6
  196.2 214.1 all-gather.8
  412.2 116.4 all-gather.10
  623.4 34.0 reduce-scatter.20
  675.4 31.7 reduce-scatter.18
  711.2 89.0 reduce-scatter.12
  804.3 232.2 reduce-scatter.16
  1040.7 156.9 reduce-scatter.10
  1201.6 264.2 reduce-scatter.14
